TPU v7x, 32 devices: a whole 2x2x4 slice. The times are simulated.
32 devices in a mesh: dp: 8 (over z, y), ctx: 4 (over x, core).
Axes of the slice: x: 2, y: 2, z: 4, core: 2. Of those that a mesh axis runs over, the one named last changes fastest.
Arguments:
- projected: bfloat16 [8, 512, 3, 4096], P('dp', 'ctx'), may hold values from -6 to 6
- short_taps: float32 [3, 3, 4096], P(None, None, 'ctx'), may hold values from -3 to 3
- long_filter: bfloat16 [512, 4096], P('dp', 'ctx'), may hold values from -1.1 to 1.1
- skip_gain: float32 [4096], P('ctx'), may hold values from -4 to 4
Outputs:
- mixed: bfloat16 [8, 512, 4096], P('dp', 'ctx')
All inputs are finite; a program needn't handle non-finite values.
Results may differ from a plain program's by a relative error of at most 0.012.
Values may be sent and summed in bfloat16 or wider, within the bound.
A program may use at most 64 MiB of HBM per device.

v0:
```python
import math
import jax
import jax.numpy as jnp
from jax import lax
from jax.sharding import PartitionSpec as P

RADIX = 64
HIGH = lax.Precision.HIGHEST


def causal_short(extended, taps, kernel_size):
    row_count = extended.shape[0] - (kernel_size - 1)
    widened = extended.astype(jnp.float32)
    summed = jnp.zeros((row_count,) + widened.shape[1:], jnp.float32)
    for tap_index in range(kernel_size):
        offset = kernel_size - 1 - tap_index
        summed = summed + taps[tap_index] * widened[offset : offset + row_count]
    return (summed[:, 0].astype(jnp.bfloat16), (summed[:, 1] * summed[:, 2]).astype(jnp.bfloat16))


def dft_tables(length, radix_size):
    outer_size = 2 * length // radix_size
    total_size = outer_size * radix_size
    outer_range = jnp.arange(outer_size, dtype=jnp.int32)
    inner_range = jnp.arange(radix_size, dtype=jnp.int32)
    angle_one = (
        2.0
        * math.pi
        / outer_size
        * (outer_range[:, None] * outer_range[None, :] % outer_size).astype(jnp.float32)
    )
    angle_twist = (
        2.0
        * math.pi
        / total_size
        * (outer_range[:, None] * inner_range[None, :] % total_size).astype(jnp.float32)
    )
    angle_two = (
        2.0
        * math.pi
        / radix_size
        * (inner_range[:, None] * inner_range[None, :] % radix_size).astype(jnp.float32)
    )
    twist_cos = jnp.cos(angle_twist)[:, :, None]
    twist_sin = jnp.sin(angle_twist)[:, :, None]
    return (
        jnp.cos(angle_one),
        jnp.sin(angle_one),
        twist_cos,
        twist_sin,
        jnp.cos(angle_two),
        jnp.sin(angle_two),
    )


def forward_dft(signal, tables, radix_size):
    cos_one, sin_one, twist_cos, twist_sin, cos_two, sin_two = tables
    outer_size = cos_one.shape[0]
    half_size = outer_size // 2
    block_width = signal.shape[1]
    shaped = signal.reshape(half_size, radix_size * block_width)
    first_re = jnp.dot(cos_one[:, :half_size], shaped, precision=HIGH).reshape(
        outer_size, radix_size, block_width
    )
    first_im = -jnp.dot(sin_one[:, :half_size], shaped, precision=HIGH).reshape(
        outer_size, radix_size, block_width
    )
    second_re = first_re * twist_cos + first_im * twist_sin
    second_im = first_im * twist_cos - first_re * twist_sin
    spec_re = jnp.einsum("amc,mb->abc", second_re, cos_two, precision=HIGH) + jnp.einsum(
        "amc,mb->abc", second_im, sin_two, precision=HIGH
    )
    spec_im = jnp.einsum("amc,mb->abc", second_im, cos_two, precision=HIGH) - jnp.einsum(
        "amc,mb->abc", second_re, sin_two, precision=HIGH
    )
    return (spec_re, spec_im)


def inverse_dft(spec_re, spec_im, tables, radix_size):
    cos_one, sin_one, twist_cos, twist_sin, cos_two, sin_two = tables
    outer_size = cos_one.shape[0]
    half_size = outer_size // 2
    block_width = spec_re.shape[2]
    back_re = jnp.einsum("abc,mb->amc", spec_re, cos_two, precision=HIGH) - jnp.einsum(
        "abc,mb->amc", spec_im, sin_two, precision=HIGH
    )
    back_im = jnp.einsum("abc,mb->amc", spec_re, sin_two, precision=HIGH) + jnp.einsum(
        "abc,mb->amc", spec_im, cos_two, precision=HIGH
    )
    turned_re = (back_re * twist_cos - back_im * twist_sin).reshape(
        outer_size, radix_size * block_width
    )
    turned_im = (back_re * twist_sin + back_im * twist_cos).reshape(
        outer_size, radix_size * block_width
    )
    result = jnp.dot(cos_one[:half_size], turned_re, precision=HIGH) - jnp.dot(
        sin_one[:half_size], turned_im, precision=HIGH
    )
    return result.reshape(half_size * radix_size, block_width) / (outer_size * radix_size)


def long_convolve(gated_slab, filter_slab):
    length, channels = gated_slab.shape
    block_width = min(128, channels)
    tables = dft_tables(length, RADIX)

    def one_block(block_index, output):
        offset = block_index * block_width
        signal = lax.dynamic_slice_in_dim(gated_slab, offset, block_width, 1).astype(jnp.float32)
        kernel_block = lax.dynamic_slice_in_dim(filter_slab, offset, block_width, 1).astype(
            jnp.float32
        )
        sig_re, sig_im = forward_dft(signal, tables, RADIX)
        ker_re, ker_im = forward_dft(kernel_block, tables, RADIX)
        prod_re = sig_re * ker_re - sig_im * ker_im
        prod_im = sig_re * ker_im + sig_im * ker_re
        result = inverse_dft(prod_re, prod_im, tables, RADIX)
        return lax.dynamic_update_slice_in_dim(output, result, offset, 1)

    return lax.fori_loop(
        0, channels // block_width, one_block, jnp.zeros((length, channels), jnp.float32)
    )


def make_response(gated_slab, filter_slab, skip_gain):
    long_part = long_convolve(gated_slab, filter_slab)
    return (long_part + skip_gain * gated_slab.astype(jnp.float32)).astype(jnp.bfloat16)


def combine_rows(query_part, response_part):
    return (query_part.astype(jnp.float32) * response_part.astype(jnp.float32)).astype(jnp.bfloat16)


def on_device(projected, short_taps, long_filter, skip_gain):
    kernel_size = short_taps.shape[0]
    tok_rows = projected[0]
    filter_slab = lax.all_gather(long_filter, "dp", axis=0, tiled=True)
    stream_slab = lax.all_to_all(tok_rows, "ctx", split_axis=2, concat_axis=0, tiled=True)
    extended = jnp.pad(stream_slab, ((kernel_size - 1, 0), (0, 0), (0, 0)))
    query_slab, gated_slab = causal_short(extended, short_taps, kernel_size)
    response_slab = make_response(gated_slab, filter_slab, skip_gain)
    mixed = lax.all_to_all(
        combine_rows(query_slab, response_slab), "ctx", split_axis=0, concat_axis=1, tiled=True
    )
    return mixed[None]


def solution(mesh):
    return jax.shard_map(
        on_device,
        mesh=mesh,
        in_specs=(P("dp", "ctx", None, None), P(None, None, "ctx"), P("dp", "ctx"), P("ctx")),
        out_specs=P("dp", "ctx", None),
        check_vma=False,
    )
```

profile of v0, /device:TPU:0, one launch (start us, length us, event | category | flops | bytes accessed | tf_op | source)
XLA Modules:
  0.0 225.1 jit_solution(1443863807638157853)
XLA Ops:
  6.5 7.2 %copy.33 = bf16[1,128,3,4096]{1,2,3,0:T(4,128)(2,1)} copy(bf16[1,128,3,4096]{3,1,2,0:T(8,128)(2,1)} %param.6) | data formatting | bytes 6291456 | tf_op args[0]
  13.8 5.0 %all-to-all-start = ((bf16[128,3,4096]{0,1,2:T(4,128)(2,1)}), bf16[128,3,4096]{0,1,2:T(4,128)(2,1)}, u32[]{:S(2)}, u32[]{:S(2)}) async-start(bf16[128,3,4096]{0,1,2:T(4,128)(2,1)} %bitcast.224), calls=%async_computation | async-start | bytes 8388608 | tf_op jit(solution)/shard_map/all_to_all | solution.py:138
  19.6 48.0 %all-to-all-done = bf16[128,3,4096]{0,1,2:T(4,128)(2,1)} async-done(((bf16[128,3,4096]{0,1,2:T(4,128)(2,1)}), bf16[128,3,4096]{0,1,2:T(4,128)(2,1)}, u32[]{:S(2)}, u32[]{:S(2)}) %all-to-all-start) | async-done | bytes 3145760 | tf_op jit(solution)/shard_map/all_to_all | solution.py:138
  67.6 5.5 %copy.34 = bf16[4,128,3,1024]{3,1,0,2:T(8,128)(2,1)S(1)} copy(bf16[4,128,3,1024]{1,2,3,0:T(4,128)(2,1)} %bitcast.3) | data formatting | bytes 6291456 | tf_op jit(solution)/shard_map/all_to_all | solution.py:138
  73.1 0.9 pad_convert_fusion
  74.0 1.9 fusion.123
  75.9 2.6 %copy-done = f32[512,3,1024]{2,0,1:T(8,128)} copy-done((f32[512,3,1024]{2,0,1:T(8,128)}, f32[512,3,1024]{2,0,1:T(8,128)S(1)}, u32[]{:S(2)}) %copy-start) | copy-done | bytes 6291480
  78.6 1.3 fusion.128
  80.1 115.5 %while.15 = (s32[]{:T(128)}, f32[512,1024]{1,0:T(8,128)S(1)}, bf16[512,1024]{1,0:T(8,128)(2,1)}, f32[16,16]{1,0:T(8,128)S(1)}, f32[16,16]{1,0:T(8,128)S(1)}, /*i...) while((s32[]{:T(128)}, f32[512,1024]{1,0:T(8,128)S(1)}, ...), condition=%wide.region_1.2_spmd.clone.clone, body=%wide.region_0.1_spmd.clone.clone.sunk | while | flops 1288484864 | bytes 33853592 | solution.py:120
  80.3 1.0 constant_dynamic-slice_fusion.3
  89.2 0.9 multiply_add_fusion.4
  92.3 0.9 multiply_add_fusion.5
  94.7 1.0 constant_dynamic-slice_fusion.3
  106.7 0.9 multiply_add_fusion.5
  109.1 1.0 constant_dynamic-slice_fusion.3
  121.1 0.9 multiply_add_fusion.5
  123.5 1.0 constant_dynamic-slice_fusion.3
  138.0 1.0 constant_dynamic-slice_fusion.3
  152.4 1.0 constant_dynamic-slice_fusion.3
  166.8 1.0 constant_dynamic-slice_fusion.3
  181.2 1.0 constant_dynamic-slice_fusion.3
  195.6 3.8 %fusion.126 = bf16[512,1024]{1,0:T(8,128)(2,1)S(1)} fusion(f32[512,1024]{1,0:T(8,128)S(1)} %get-tuple-element.246, f32[512,3,1024]{2,0,1:T(8,128)} %copy-done, f32[1024]{0:T(1024)S(1)} %copy-done.2), kind=kLoop, calls=%fused_computation.151 | loop fusion | flops 5242880 | bytes 8392704 | tf_op jit(solution)/shard_map/convert_element_type | solution.py:131
  199.4 16.9 %all_to_all.34 = bf16[4,128,1024]{2,1,0:T(8,128)(2,1)S(1)} all-to-all(bf16[4,128,1024]{2,1,0:T(8,128)(2,1)S(1)} %bitcast.227), channel_id=1, replica_groups=mesh['dp'=8,'ctx'=4] {'ctx'}, dimensions={0} | all-to-all | bytes 2097152 | tf_op jit(solution)/shard_map/all_to_all | solution.py:142
  217.0 1.3 copy.36
  (232 shorter events, 103.5 us)
Async XLA Ops:
  13.8 5.8 %copy-start.1 = (f32[3,3,1024]{2,1,0:T(4,128)S(1)}, f32[3,3,1024]{2,1,0:T(4,128)}, u32[]{:S(2)}) copy-start(f32[3,3,1024]{2,1,0:T(4,128)} %param.7) | copy-start | bytes 110596
  13.8 53.8 %all-to-all-start = ((bf16[128,3,4096]{0,1,2:T(4,128)(2,1)}), bf16[128,3,4096]{0,1,2:T(4,128)(2,1)}, u32[]{:S(2)}, u32[]{:S(2)}) async-start(bf16[128,3,4096]{0,1,2:T(4,128)(2,1)} %bitcast.224), calls=%async_computation | async-start | bytes 8388608 | tf_op jit(solution)/shard_map/all_to_all | solution.py:138
  18.7 61.1 %all-gather.2.cloned.1.call-start = ((), (), s32[]{:S(2)}) async-start(), calls=%async_computation.2 | async-start | bytes 1179648 | tf_op jit(solution)/shard_map/all_gather | solution.py:137
  75.9 2.7 %copy-start = (f32[512,3,1024]{2,0,1:T(8,128)}, f32[512,3,1024]{2,0,1:T(8,128)S(1)}, u32[]{:S(2)}) copy-start(f32[512,3,1024]{2,0,1:T(8,128)S(1)} %fusion.123) | copy-start | bytes 18874372
  80.1 115.5 %copy-start.2 = (f32[1024]{0:T(1024)S(1)}, f32[1024]{0:T(1024)}, u32[]{:S(2)}) copy-start(f32[1024]{0:T(1024)} %param.9) | copy-start | bytes 12292
Sparse Core Ops, SparseCore 0:
  21.7 43.2 all-gather.1
where the time goes:
time: 226 us; the launch traced here: 225 us
  matrix products  96.6 us (43%)
  waiting for transfers between devices  48.7 us (22%)
  local copies, waits for them, and re-layouts  30.4 us (13%)
  blocking collectives  16.9 us (7%)
  between operations  13.5 us (6%)
  other arithmetic  11.9 us (5%)
  starting transfers between devices  5.02 us (2%)
    all_to_all x1, waiting for transfers between devices, on_device(): lax.all_to_all(tok_rows, 'ctx', split_axis=2, concat_axis=0, tiled=True)  48 us
    all_to_all x1, blocking collectives, on_device(): lax.all_to_all(combine_rows(query_slab, response_slab), 'ctx', split_axis...  16.9 us
    dot_general x16, matrix products, forward_dft(): jnp.einsum('amc,mb->abc', second_re, sin_two, precision=HIGH)  13.3 us
    dot_general x16, matrix products, forward_dft(): jnp.einsum('amc,mb->abc', second_im, sin_two, precision=HIGH)  12.1 us
    dot_general x16, matrix products, forward_dft(): jnp.einsum('amc,mb->abc', second_re, cos_two, precision=HIGH)  12 us
    dot_general x16, matrix products, forward_dft(): jnp.einsum('amc,mb->abc', second_im, cos_two, precision=HIGH)  12 us
    unnamed x7, local copies, waits for them, and re-layouts  9.88 us
    dynamic_slice x8, local copies, waits for them, and re-layouts, one_block(): lax.dynamic_slice_in_dim(filter_slab, offset, block_width, 1)  7.97 us
  transfers between devices with their start and end apart: 2, of which 1 were waited for; matrix products, arithmetic and copies ran while one was open for 4% of the time, Pallas kernels for 0%

commit v1 on v0

--- a/solution.py
+++ b/solution.py
@@ -135,7 +135,10 @@
     kernel_size = short_taps.shape[0]
     tok_rows = projected[0]
     filter_slab = lax.all_gather(long_filter, "dp", axis=0, tiled=True)
-    stream_slab = lax.all_to_all(tok_rows, "ctx", split_axis=2, concat_axis=0, tiled=True)
+    stream_slab = jnp.concatenate(
+        lax.all_to_all(jnp.stack(jnp.split(tok_rows, lax.axis_size("ctx"), axis=2)), "ctx", 0, 0),
+        axis=0,
+    )
     extended = jnp.pad(stream_slab, ((kernel_size - 1, 0), (0, 0), (0, 0)))
     query_slab, gated_slab = causal_short(extended, short_taps, kernel_size)
     response_slab = make_response(gated_slab, filter_slab, skip_gain)

time: 226 us -> 207 us (0.916)
  waiting for transfers between devices: 48.7 us -> 38.5 us
  local copies, waits for them, and re-layouts: 30.4 us -> 20.2 us
    all_to_all x1, waiting for transfers between devices: 48 us -> 36.2 us  [on_device(): lax.all_to_all(jnp.stack(jnp.split(tok_rows, lax.axis_size('ctx'), axis=2...]
    unnamed x7 -> x6, local copies, waits for them, and re-layouts: 9.88 us -> 2.67 us
    all_to_all x1, local copies, waits for them, and re-layouts: 5.51 us -> 0.35 us  [on_device(): lax.all_to_all(jnp.stack(jnp.split(tok_rows, lax.axis_size('ctx'), axis=2...]
  transfers between devices with their start and end apart: 2 -> 2, of which waited for: 1 -> 2; matrix products, arithmetic and copies ran while one was open for 4% -> 2% of each run, Pallas kernels for 0% -> 0%
where the time goes in v1:
time: 207 us; the launch traced here: 206 us
  matrix products  96.6 us (47%)
  waiting for transfers between devices  38.5 us (19%)
  local copies, waits for them, and re-layouts  20.2 us (10%)
  blocking collectives  17 us (8%)
  other arithmetic  13.8 us (7%)
  between operations  13.5 us (7%)
  starting transfers between devices  4.34 us (2%)
    all_to_all x1, waiting for transfers between devices, on_device(): lax.all_to_all(jnp.stack(jnp.split(tok_rows, lax.axis_size('ctx'), axis=2...  36.2 us
    all_to_all x1, blocking collectives, on_device(): lax.all_to_all(combine_rows(query_slab, response_slab), 'ctx', split_axis...  17 us
    dot_general x16, matrix products, forward_dft(): jnp.einsum('amc,mb->abc', second_re, sin_two, precision=HIGH)  13.3 us
    dot_general x16, matrix products, forward_dft(): jnp.einsum('amc,mb->abc', second_im, sin_two, precision=HIGH)  12.1 us
    dot_general x16, matrix products, forward_dft(): jnp.einsum('amc,mb->abc', second_re, cos_two, precision=HIGH)  12 us
    dot_general x16, matrix products, forward_dft(): jnp.einsum('amc,mb->abc', second_im, cos_two, precision=HIGH)  12 us
    dynamic_slice x8, local copies, waits for them, and re-layouts, one_block(): lax.dynamic_slice_in_dim(filter_slab, offset, block_width, 1)  7.97 us
    dot_general x8, matrix products, inverse_dft(): jnp.einsum('abc,mb->amc', spec_im, cos_two, precision=HIGH)  7.17 us
  transfers between devices with their start and end apart: 2, of which 2 were waited for; matrix products, arithmetic and copies ran while one was open for 2% of the time, Pallas kernels for 0%

profile of v1, /device:TPU:0, one launch (start us, length us, event | category | flops | bytes accessed | tf_op | source)
XLA Modules:
  0.0 206.1 jit_solution(3456944928402386581)
XLA Ops:
  6.5 2.2 %slice_bitcast_fusion.3 = (bf16[1,128,3,1024]{3,1,2,0:T(8,128)(2,1)S(1)}, bf16[1,128,3,1024]{3,1,2,0:T(8,128)(2,1)S(1)}, bf16[1,128,3,1024]{3,1,2,0:T(8,128)(2,1)S(1)}, bf16[1,128,3,1024]{3,1,2,0:T(8,128)(2,1)S(1)}) fusion(bf16[128,3,4096]{2,0,1:T(8,128)(2,1)} %bitcast.232), kind=kLoop, calls=%fused_computation.159 | loop fusion | bytes 6291456 | tf_op jit(solution)/shard_map/stack | solution.py:139
  8.7 1.9 pad_maximum_fusion
  10.6 4.3 %all-to-all-start = ((bf16[4,128,3,1024]{3,1,2,0:T(8,128)(2,1)}), bf16[4,128,3,1024]{3,1,2,0:T(8,128)(2,1)S(1)}, u32[]{:S(2)}, u32[]{:S(2)}) async-start(bf16[4,128,3,1024]{3,1,2,0:T(8,128)(2,1)} %pad_maximum_fusion), calls=%async_computation | async-start | bytes 6291456 | tf_op jit(solution)/shard_map/all_to_all | solution.py:139
  15.7 36.2 %all-to-all-done = bf16[4,128,3,1024]{3,1,2,0:T(8,128)(2,1)S(1)} async-done(((bf16[4,128,3,1024]{3,1,2,0:T(8,128)(2,1)}), bf16[4,128,3,1024]{3,1,2,0:T(8,128)(2,1)S(1)}, u32[]{:S(2)}, u32[]{:S(2)}) %all-to-all-start) | async-done | bytes 3145760 | tf_op jit(solution)/shard_map/all_to_all | solution.py:139
  52.2 0.9 pad_convert_fusion
  53.2 1.9 fusion.123
  55.1 2.7 %copy-done = f32[512,3,1024]{2,0,1:T(8,128)} copy-done((f32[512,3,1024]{2,0,1:T(8,128)}, f32[512,3,1024]{2,0,1:T(8,128)S(1)}, u32[]{:S(2)}) %copy-start) | copy-done | bytes 6291480
  57.7 1.3 fusion.128
  59.0 1.6 all-gather.2.cloned.1.call-done
  60.9 115.5 %while.15 = (s32[]{:T(128)}, f32[512,1024]{1,0:T(8,128)S(1)}, bf16[512,1024]{1,0:T(8,128)(2,1)}, f32[16,16]{1,0:T(8,128)S(1)}, f32[16,16]{1,0:T(8,128)S(1)}, /*i...) while((s32[]{:T(128)}, f32[512,1024]{1,0:T(8,128)S(1)}, ...), condition=%wide.region_1.2_spmd.clone.clone, body=%wide.region_0.1_spmd.clone.clone.sunk | while | flops 1288484864 | bytes 33853592 | solution.py:120
  61.1 1.0 constant_dynamic-slice_fusion.3
  73.1 0.9 multiply_add_fusion.5
  75.5 1.0 constant_dynamic-slice_fusion.3
  87.5 0.9 multiply_add_fusion.5
  89.9 1.0 constant_dynamic-slice_fusion.3
  98.8 0.9 multiply_add_fusion.4
  104.4 1.0 constant_dynamic-slice_fusion.3
  118.8 1.0 constant_dynamic-slice_fusion.3
  133.2 1.0 constant_dynamic-slice_fusion.3
  147.6 1.0 constant_dynamic-slice_fusion.3
  162.0 1.0 constant_dynamic-slice_fusion.3
  176.5 3.8 %fusion.126 = bf16[512,1024]{1,0:T(8,128)(2,1)S(1)} fusion(f32[512,1024]{1,0:T(8,128)S(1)} %get-tuple-element.246, f32[512,3,1024]{2,0,1:T(8,128)} %copy-done, f32[1024]{0:T(1024)S(1)} %copy-done.2), kind=kLoop, calls=%fused_computation.152 | loop fusion | flops 5242880 | bytes 8392704 | tf_op jit(solution)/shard_map/convert_element_type | solution.py:131
  180.3 17.0 %all_to_all.21 = bf16[4,128,1024]{2,1,0:T(8,128)(2,1)S(1)} all-to-all(bf16[4,128,1024]{2,1,0:T(8,128)(2,1)S(1)} %bitcast.231), channel_id=1, replica_groups=mesh['dp'=8,'ctx'=4] {'ctx'}, dimensions={0} | all-to-all | bytes 2097152 | tf_op jit(solution)/shard_map/all_to_all | solution.py:145
  198.0 1.3 copy.34
  (233 shorter events, 104.8 us)
Async XLA Ops:
  10.5 5.1 %copy-start.1 = (f32[3,3,1024]{2,1,0:T(4,128)S(1)}, f32[3,3,1024]{2,1,0:T(4,128)}, u32[]{:S(2)}) copy-start(f32[3,3,1024]{2,1,0:T(4,128)} %param.7) | copy-start | bytes 110596
  10.6 41.3 %all-to-all-start = ((bf16[4,128,3,1024]{3,1,2,0:T(8,128)(2,1)}), bf16[4,128,3,1024]{3,1,2,0:T(8,128)(2,1)S(1)}, u32[]{:S(2)}, u32[]{:S(2)}) async-start(bf16[4,128,3,1024]{3,1,2,0:T(8,128)(2,1)} %pad_maximum_fusion), calls=%async_computation | async-start | bytes 6291456 | tf_op jit(solution)/shard_map/all_to_all | solution.py:139
  14.9 45.8 %all-gather.2.cloned.1.call-start = ((), (), s32[]{:S(2)}) async-start(), calls=%async_computation.2 | async-start | bytes 1179648 | tf_op jit(solution)/shard_map/all_gather | solution.py:137
  55.1 2.7 %copy-start = (f32[512,3,1024]{2,0,1:T(8,128)}, f32[512,3,1024]{2,0,1:T(8,128)S(1)}, u32[]{:S(2)}) copy-start(f32[512,3,1024]{2,0,1:T(8,128)S(1)} %fusion.123) | copy-start | bytes 18874372
  60.9 115.5 %copy-start.2 = (f32[1024]{0:T(1024)S(1)}, f32[1024]{0:T(1024)}, u32[]{:S(2)}) copy-start(f32[1024]{0:T(1024)} %param.9) | copy-start | bytes 12292
Sparse Core Ops, SparseCore 0:
  17.8 42.7 all-gather.1
